TPU v7x, 32 devices: a whole 2x2x4 slice. The times are simulated.
32 devices in a mesh: dp: 16 (over z, x, core), tensor: 2 (over y).
Axes of the slice: x: 2, y: 2, z: 4, core: 2. Of those that a mesh axis runs over, the one named last changes fastest.
Arguments:
- hidden: bfloat16 [2, 16384, 768], P(None, ('dp', 'tensor')), may hold values from -6 to 6
- lengths: int32 [2, 16], P(None, 'dp'), may hold values from 256 to 1024, as said below
- cotangent: bfloat16 [2, 16384, 768], P(None, ('dp', 'tensor')), may hold values from -6 to 6
- w_query: bfloat16 [768, 768], P('dp', 'tensor'), may hold values from -0.21875 to 0.21875
- w_key: bfloat16 [768, 768], P('dp', 'tensor'), may hold values from -0.21875 to 0.21875
- w_value: bfloat16 [768, 768], P('dp', 'tensor'), may hold values from -0.21875 to 0.21875
- w_out: bfloat16 [768, 768], P('dp', 'tensor'), may hold values from -1.5 to 1.5
- w_in: bfloat16 [768, 3072], P('dp', 'tensor'), may hold values from -0.21875 to 0.21875
- w_back: bfloat16 [768, 3072], P('dp', 'tensor'), may hold values from -0.109375 to 0.109375
- b_query: float32 [768], replicated, may hold values from -1.75 to 1.75
- b_value: float32 [768], replicated, may hold values from -0.3125 to 0.3125
- b_out: float32 [768], replicated, may hold values from -1.75 to 1.75
- b_in: float32 [3072], replicated, may hold values from -1.75 to 1.75
- b_back: float32 [768], replicated, may hold values from -1.75 to 1.75
- gain_one: float32 [768], replicated, may hold values from 0.5 to 1.5
- shift_one: float32 [768], replicated, may hold values from -1.75 to 1.75
- gain_two: float32 [768], replicated, may hold values from 0.5 to 1.5
- shift_two: float32 [768], replicated, may hold values from -1.75 to 1.75
Outputs:
- output: bfloat16 [2, 16384, 768], P(None, ('dp', 'tensor'))
- grad_hidden: bfloat16 [2, 16384, 768], P(None, ('dp', 'tensor'))
- grad_w_query: float32 [768, 768], P('dp', 'tensor')
- grad_w_key: float32 [768, 768], P('dp', 'tensor')
- grad_w_value: float32 [768, 768], P('dp', 'tensor')
- grad_w_out: float32 [768, 768], P('dp', 'tensor')
- grad_w_in: float32 [768, 3072], P('dp', 'tensor')
- grad_w_back: float32 [768, 3072], P('dp', 'tensor')
- grad_b_query: float32 [768], replicated
- grad_b_value: float32 [768], replicated
- grad_b_out: float32 [768], replicated
- grad_b_in: float32 [3072], replicated
- grad_b_back: float32 [768], replicated
- grad_gain_one: float32 [768], replicated
- grad_shift_one: float32 [768], replicated
- grad_gain_two: float32 [768], replicated
- grad_shift_two: float32 [768], replicated
Inputs may be any that keep to these rules, and one draw needn't show every extreme that they name: `lengths`: the count of real tokens of each sequence; its other slots of 1024 are padding. Some sequence has exactly 1024 and some exactly 256.
All inputs are finite; a program needn't handle non-finite values.
Results may differ from a plain program's by a relative error of at most 0.017.
Values may be sent and summed in bfloat16 or wider, within the bound.
A program may use at most 192 MiB of HBM per device.

v0:
```python
import math
import jax
import jax.numpy as jnp
from jax import lax
from jax.sharding import PartitionSpec as P

DH = 64


def layer_norm(values, gain_vec, shift_vec):
    center = values - jnp.mean(values, axis=-1, keepdims=True)
    spread = jnp.mean(center * center, axis=-1, keepdims=True)
    return center * lax.rsqrt(spread + 1e-05) * gain_vec + shift_vec


def gelu_exact(values):
    return jax.nn.gelu(values, approximate=False)


def product(left_side, right_side):
    return jnp.dot(left_side, right_side, preferred_element_type=jnp.float32)


def contract_last(left_side, right_side):
    return lax.dot_general(
        left_side, right_side, (((1,), (1,)), ((), ())), preferred_element_type=jnp.float32
    )


def contract_first(left_side, right_side):
    return lax.dot_general(
        left_side, right_side, (((0,), (0,)), ((), ())), preferred_element_type=jnp.float32
    )


def fetch_weights(w_query, w_key, w_value, w_out, w_in, w_back):
    return (
        lax.all_gather(w_query, "dp", axis=0, tiled=True),
        lax.all_gather(w_key, "dp", axis=0, tiled=True),
        lax.all_gather(w_value, "dp", axis=0, tiled=True),
        lax.all_gather(w_out, "dp", axis=0, tiled=True),
        lax.all_gather(w_in, "dp", axis=0, tiled=True),
        lax.all_gather(w_back, "dp", axis=0, tiled=True),
    )


def reduce_weights(grad_query, grad_key, grad_value, grad_out, grad_in, grad_back):
    return (
        lax.psum_scatter(grad_query, "dp", scatter_dimension=0, tiled=True),
        lax.psum_scatter(grad_key, "dp", scatter_dimension=0, tiled=True),
        lax.psum_scatter(grad_value, "dp", scatter_dimension=0, tiled=True),
        lax.psum_scatter(grad_out, "dp", scatter_dimension=0, tiled=True),
        lax.psum_scatter(grad_in, "dp", scatter_dimension=0, tiled=True),
        lax.psum_scatter(grad_back, "dp", scatter_dimension=0, tiled=True),
    )


def head_slice(matrix, head_index):
    return lax.dynamic_slice_in_dim(matrix, head_index * DH, DH, 1)


def side_by_side(stacked):
    return jnp.transpose(stacked, (1, 0, 2)).reshape(
        stacked.shape[1], stacked.shape[0] * stacked.shape[2]
    )


def attend_forward(query_rows, key_rows, value_rows, key_live, block_rows):
    seq_len = query_rows.shape[0]
    head_count = query_rows.shape[1] // DH
    scaling = 1.0 / math.sqrt(DH)

    def one_head(head_index):
        query_head = head_slice(query_rows, head_index)
        key_head = head_slice(key_rows, head_index)
        value_head = head_slice(value_rows, head_index)
        outputs = []
        log_parts = []
        for row_first in range(0, seq_len, block_rows):
            query_block = query_head[row_first : row_first + block_rows]
            scores = jnp.where(
                key_live[None, :], contract_last(query_block, key_head) * scaling, -1000000000.0
            )
            row_max = jnp.max(scores, axis=1, keepdims=True)
            exponent = jnp.exp(scores - row_max)
            row_total = jnp.sum(exponent, axis=1, keepdims=True)
            probs_low = (exponent / row_total).astype(jnp.bfloat16)
            outputs.append(product(probs_low, value_head))
            log_parts.append((row_max + jnp.log(row_total))[:, 0])
        return (jnp.concatenate(outputs, 0), jnp.concatenate(log_parts, 0))

    attended, log_sums = lax.map(one_head, jnp.arange(head_count, dtype=jnp.int32))
    return (side_by_side(attended).astype(jnp.bfloat16), log_sums)


def attend_backward(
    query_rows, key_rows, value_rows, log_sums, grad_attended, key_live, block_rows
):
    seq_len = query_rows.shape[0]
    head_count = query_rows.shape[1] // DH
    scaling = 1.0 / math.sqrt(DH)

    def one_head(head_index):
        query_head = head_slice(query_rows, head_index)
        key_head = head_slice(key_rows, head_index)
        value_head = head_slice(value_rows, head_index)
        grad_head = head_slice(grad_attended, head_index)
        log_head = log_sums[head_index]
        grad_keys = jnp.zeros(key_head.shape, jnp.float32)
        grad_values = jnp.zeros(value_head.shape, jnp.float32)
        grad_queries = []
        for row_first in range(0, seq_len, block_rows):
            query_block = query_head[row_first : row_first + block_rows]
            grad_block = grad_head[row_first : row_first + block_rows]
            log_block = log_head[row_first : row_first + block_rows]
            scores = jnp.where(
                key_live[None, :], contract_last(query_block, key_head) * scaling, -1000000000.0
            )
            soft_weights = jnp.exp(scores - log_block[:, None])
            probs_low = soft_weights.astype(jnp.bfloat16)
            grad_probs = contract_last(grad_block, value_head)
            weighted = jnp.sum(soft_weights * grad_probs, axis=1, keepdims=True)
            grad_scores = (soft_weights * (grad_probs - weighted)).astype(jnp.bfloat16)
            grad_queries.append((product(grad_scores, key_head) * scaling).astype(jnp.bfloat16))
            grad_keys = grad_keys + contract_first(grad_scores, query_block) * scaling
            grad_values = grad_values + contract_first(probs_low, grad_block)
        return (
            jnp.concatenate(grad_queries, 0),
            grad_keys.astype(jnp.bfloat16),
            grad_values.astype(jnp.bfloat16),
        )

    grad_query, grad_key, grad_value = lax.map(one_head, jnp.arange(head_count, dtype=jnp.int32))
    return (side_by_side(grad_query), side_by_side(grad_key), side_by_side(grad_value))


def widen_vector(vector, full_size, tensor_index):
    empty_vector = jnp.zeros((full_size,), jnp.float32)
    return lax.dynamic_update_slice(empty_vector, vector, (tensor_index * vector.shape[0],))


def per_device(
    hidden,
    lengths,
    cotangent,
    w_query,
    w_key,
    w_value,
    w_out,
    w_in,
    w_back,
    b_query,
    b_value,
    b_out,
    b_in,
    b_back,
    gain_one,
    shift_one,
    gain_two,
    shift_two,
):
    micro_count = hidden.shape[0]
    local_rows = hidden.shape[1]
    tensor_index = lax.axis_index("tensor")
    model_width = b_query.shape[0]
    inner_width = b_in.shape[0]
    seq_len = local_rows * lax.axis_size("tensor")
    block_rows = min(512, seq_len)
    half_width = w_query.shape[1]
    half_inner = w_in.shape[1]
    query_bias = lax.dynamic_slice_in_dim(b_query, tensor_index * half_width, half_width)
    value_bias = lax.dynamic_slice_in_dim(b_value, tensor_index * half_width, half_width)
    inner_bias = lax.dynamic_slice_in_dim(b_in, tensor_index * half_inner, half_inner)
    row_place = tensor_index * local_rows + jnp.arange(local_rows, dtype=jnp.int32)
    key_place = jnp.arange(seq_len, dtype=jnp.int32)
    outputs = []
    grad_rows = []
    owned_grads = None
    small_sums = None
    for micro_index in range(micro_count):
        gathered = fetch_weights(w_query, w_key, w_value, w_out, w_in, w_back)
        full_query, full_key, full_value, full_out, full_in, full_back = gathered
        length = lengths[micro_index, 0]
        key_live = key_place < length
        rows_in = hidden[micro_index]
        rows_f32 = rows_in.astype(jnp.float32)
        full_rows = lax.all_gather(rows_in, "tensor", axis=0, tiled=True)
        query_rows = (product(full_rows, full_query) + query_bias).astype(jnp.bfloat16)
        key_rows = product(full_rows, full_key).astype(jnp.bfloat16)
        value_rows = (product(full_rows, full_value) + value_bias).astype(jnp.bfloat16)
        attended, log_sums = attend_forward(query_rows, key_rows, value_rows, key_live, block_rows)
        branch_one = lax.psum_scatter(
            contract_last(
                lax.slice_in_dim(attended, 0, local_rows * lax.axis_size("tensor"), axis=0),
                full_out,
            ),
            "tensor",
            scatter_dimension=0,
            tiled=True,
        )
        sum_one = rows_f32 + branch_one + b_out
        normed_one, pull_one = jax.vjp(layer_norm, sum_one, gain_one, shift_one)
        mid_rows = lax.all_gather(normed_one.astype(jnp.bfloat16), "tensor", axis=0, tiled=True)
        hidden_pre = product(mid_rows, full_in) + inner_bias
        active_f32, pull_gelu = jax.vjp(gelu_exact, hidden_pre)
        active = active_f32.astype(jnp.bfloat16)
        branch_two = lax.psum_scatter(
            contract_last(active, full_back).astype(jnp.bfloat16),
            "tensor",
            scatter_dimension=0,
            tiled=True,
        ).astype(jnp.float32)
        sum_two = normed_one + branch_two + b_back
        result, pull_two = jax.vjp(layer_norm, sum_two, gain_two, shift_two)
        outputs.append(result.astype(jnp.bfloat16))
        row_live = (row_place < length).astype(jnp.float32)
        grad_out = cotangent[micro_index].astype(jnp.float32) * row_live[:, None]
        grad_two, grad_gain_two, grad_shift_two = pull_two(grad_out)
        back_rows = lax.all_gather(grad_two.astype(jnp.bfloat16), "tensor", axis=0, tiled=True)
        grad_w_back = contract_first(back_rows, active)
        grad_active = product(back_rows, full_back)
        grad_pre = pull_gelu(grad_active)[0].astype(jnp.bfloat16)
        grad_w_in = contract_first(mid_rows, grad_pre)
        grad_normed = (
            lax.psum_scatter(
                contract_last(grad_pre, full_in).astype(jnp.bfloat16),
                "tensor",
                scatter_dimension=0,
                tiled=True,
            ).astype(jnp.float32)
            + grad_two
        )
        grad_one, grad_gain_one, grad_shift_one = pull_one(grad_normed)
        attn_rows = lax.all_gather(grad_one.astype(jnp.bfloat16), "tensor", axis=0, tiled=True)
        grad_w_out = contract_first(attn_rows, attended)
        grad_attended = product(attn_rows, full_out).astype(jnp.bfloat16)
        grad_query, grad_key, grad_value = attend_backward(
            query_rows, key_rows, value_rows, log_sums, grad_attended, key_live, block_rows
        )
        grad_w_query = contract_first(full_rows, grad_query)
        grad_w_key = contract_first(full_rows, grad_key)
        grad_w_value = contract_first(full_rows, grad_value)
        total_term = contract_last(
            lax.slice_in_dim(grad_query, 0, local_rows * lax.axis_size("tensor"), axis=0),
            full_query,
        )
        total_term = total_term + contract_last(
            lax.slice_in_dim(grad_key, 0, local_rows * lax.axis_size("tensor"), axis=0), full_key
        )
        grad_input = (
            lax.psum_scatter(
                (
                    total_term
                    + contract_last(
                        lax.slice_in_dim(
                            grad_value, 0, local_rows * lax.axis_size("tensor"), axis=0
                        ),
                        full_value,
                    )
                ).astype(jnp.bfloat16),
                "tensor",
                scatter_dimension=0,
                tiled=True,
            ).astype(jnp.float32)
            + grad_one
        )
        grad_rows.append(grad_input.astype(jnp.bfloat16))
        summed = reduce_weights(
            grad_w_query, grad_w_key, grad_w_value, grad_w_out, grad_w_in, grad_w_back
        )
        owned_grads = summed if owned_grads is None else jax.tree.map(jnp.add, owned_grads, summed)
        vectors = (
            jnp.sum(grad_query.astype(jnp.float32), axis=0),
            jnp.sum(grad_value.astype(jnp.float32), axis=0),
            jnp.sum(grad_one, axis=0),
            jnp.sum(grad_pre.astype(jnp.float32), axis=0),
            jnp.sum(grad_two, axis=0),
            grad_gain_one,
            grad_shift_one,
            grad_gain_two,
            grad_shift_two,
        )
        small_sums = vectors if small_sums is None else jax.tree.map(jnp.add, small_sums, vectors)
    output_rows = jnp.stack(outputs, 0)
    grad_hidden_rows = jnp.stack(grad_rows, 0)
    small_vectors = (
        widen_vector(small_sums[0], model_width, tensor_index),
        widen_vector(small_sums[1], model_width, tensor_index),
        small_sums[2],
        widen_vector(small_sums[3], inner_width, tensor_index),
        small_sums[4],
        small_sums[5],
        small_sums[6],
        small_sums[7],
        small_sums[8],
    )
    totals = lax.psum(
        (
            small_vectors[0],
            small_vectors[1],
            small_vectors[2],
            small_vectors[3],
            small_vectors[4],
            small_vectors[5],
            small_vectors[6],
            small_vectors[7],
            small_vectors[8],
        ),
        ("dp", "tensor"),
    )
    return (
        output_rows,
        grad_hidden_rows,
        owned_grads[0],
        owned_grads[1],
        owned_grads[2],
        owned_grads[3],
        owned_grads[4],
        owned_grads[5],
        totals[0],
        totals[1],
        totals[2],
        totals[3],
        totals[4],
        totals[5],
        totals[6],
        totals[7],
        totals[8],
    )


def solution(mesh):
    return jax.shard_map(
        per_device,
        mesh=mesh,
        in_specs=(
            P(None, ("dp", "tensor"), None),
            P(None, "dp"),
            P(None, ("dp", "tensor"), None),
            P("dp", "tensor"),
            P("dp", "tensor"),
            P("dp", "tensor"),
            P("dp", "tensor"),
            P("dp", "tensor"),
            P("dp", "tensor"),
            P(),
            P(),
            P(),
            P(),
            P(),
            P(),
            P(),
            P(),
            P(),
        ),
        out_specs=(
            P(None, ("dp", "tensor"), None),
            P(None, ("dp", "tensor"), None),
            P("dp", "tensor"),
            P("dp", "tensor"),
            P("dp", "tensor"),
            P("dp", "tensor"),
            P("dp", "tensor"),
            P("dp", "tensor"),
            P(),
            P(),
            P(),
            P(),
            P(),
            P(),
            P(),
            P(),
            P(),
        ),
        check_vma=False,
    )
```

profile of v0, /device:TPU:0, one launch (start us, length us, event | category | flops | bytes accessed | tf_op | source)
XLA Modules:
  0.0 1236.6 jit_solution(3482107749326957179)
XLA Ops:
  12.3 24.8 %all_gather.49 = bf16[768,384]{1,0:T(8,128)(2,1)S(1)} all-gather(bf16[48,384]{1,0:T(8,128)(2,1)S(1)} %copy-done.51), channel_id=1, replica_groups=mesh['dp'=16,'tensor'=2] {'dp'}, dimensions={0}, use_global_device_ids=true | all-gather | bytes 626688 | tf_op jit(solution)/shard_map/all_gather | solution.py:38
  37.1 19.0 %all_gather.50 = bf16[768,384]{1,0:T(8,128)(2,1)S(1)} all-gather(bf16[48,384]{1,0:T(8,128)(2,1)S(1)} %copy-done.52), channel_id=1, replica_groups=mesh['dp'=16,'tensor'=2] {'dp'}, dimensions={0}, use_global_device_ids=true | all-gather | bytes 626688 | tf_op jit(solution)/shard_map/all_gather | solution.py:39
  56.2 20.4 %all_gather.51 = bf16[768,384]{1,0:T(8,128)(2,1)S(1)} all-gather(bf16[48,384]{1,0:T(8,128)(2,1)S(1)} %copy-done.53), channel_id=1, replica_groups=mesh['dp'=16,'tensor'=2] {'dp'}, dimensions={0}, use_global_device_ids=true | all-gather | bytes 626688 | tf_op jit(solution)/shard_map/all_gather | solution.py:40
  76.6 20.4 %all_gather.52 = bf16[768,384]{1,0:T(8,128)(2,1)} all-gather(bf16[48,384]{1,0:T(8,128)(2,1)S(1)} %copy-done.54), channel_id=1, replica_groups=mesh['dp'=16,'tensor'=2] {'dp'}, dimensions={0}, use_global_device_ids=true | all-gather | bytes 626688 | tf_op jit(solution)/shard_map/all_gather | solution.py:41
  103.2 60.1 %while.56 = (s32[]{:T(128)}, bf16[6,1024,64]{1,2,0:T(8,128)(2,1)}, f32[6,1024]{1,0:T(8,128)}, s32[6]{0:T(128)S(1)}, bf16[1024,384]{1,0:T(8,128)(2,1)S(1)}, /*ind...) while((s32[]{:T(128)}, bf16[6,1024,64]{1,2,0:T(8,128)(2,1)}, ...), condition=%wide.region_5.6_spmd.clone, body=%wide.region_0.5_spmd.clone.sunk | while | flops 281281536 | bytes 14344927 | solution.py:92
  173.7 35.8 %while.57 = (s32[]{:T(128)}, bf16[6,1024,64]{1,2,0:T(8,128)(2,1)S(1)}, f32[6,1024]{1,0:T(8,128)S(1)}, s32[6]{0:T(128)S(1)}, bf16[1024,384]{1,0:T(8,128)(2,1)S(1)...) while((s32[]{:T(128)}, ...), condition=%wide.region_17.18_spmd.clone, body=%wide.region_12.0_spmd.clone.sunk | while | flops 281281536 | bytes 14344927 | solution.py:92
  214.5 41.4 %reduce-scatter.25.cloned.1.call-done = f32[512,768]{1,0:T(8,128)} async-done(((f32[1024,768]{1,0:T(8,128)}), f32[512,768]{1,0:T(8,128)}) %reduce-scatter.25.cloned.1.call-update) | async-done | bytes 1572880 | tf_op jit(solution)/shard_map/reduce_scatter | solution.py:192
  263.3 25.5 %all-gather.19.cloned.1.call-done = bf16[1024,768]{1,0:T(8,128)(2,1)} async-done(((bf16[512,768]{1,0:T(8,128)(2,1)}), bf16[1024,768]{1,0:T(8,128)(2,1)}) %all-gather.19.cloned.1.call-update) | async-done | bytes 1572880 | tf_op jit(solution)/shard_map/all_gather | solution.py:203
  296.2 21.7 %all-gather.13.cloned.1.call-done = bf16[1024,768]{1,0:T(8,128)(2,1)} async-done(((bf16[512,768]{1,0:T(8,128)(2,1)}), bf16[1024,768]{1,0:T(8,128)(2,1)}) %all-gather.13.cloned.1.call-update) | async-done | bytes 1572880 | tf_op jit(solution)/shard_map/all_gather | solution.py:203
  317.9 32.9 %multiply_convert_fusion.5 = (bf16[1024,1536]{1,0:T(8,128)(2,1)}, f32[1024,1536]{1,0:T(8,128)}, bf16[1024,1536]{1,0:T(8,128)(2,1)}, f32[1024,1536]{1,0:T(8,128)}, f32[1024,1536]{1,0:T(8,128)}) fusion(f32[1536]{0:T(1024)S(1)} %dynamic_slice.72, f32[1024,1536]{1,0:T(8,128)} %fusion.246, bf16[1024,768]{1,0:T(8,128)(2,1)} %all-gather.13.cloned.1.call-done, ...), kind=kOutput, calls=%fused_computation.195 | convolution fusion | flops 2623537152 | bytes 35395584 | tf_op jit(solution)/shard_map/dot_general | solution.py:21
  393.9 28.9 %reduce-scatter.27.cloned.1.call-done = bf16[512,768]{1,0:T(8,128)(2,1)} async-done(((bf16[1024,768]{1,0:T(8,128)(2,1)}), bf16[512,768]{1,0:T(8,128)(2,1)}) %reduce-scatter.27.cloned.1.call-update) | async-done | bytes 786448 | tf_op jit(solution)/shard_map/reduce_scatter | solution.py:207
  436.6 24.8 %all-gather.25.cloned.1.call-done = bf16[1024,768]{1,0:T(8,128)(2,1)} async-done(((bf16[512,768]{1,0:T(8,128)(2,1)}), bf16[1024,768]{1,0:T(8,128)(2,1)}) %all-gather.25.cloned.1.call-update) | async-done | bytes 1572880 | tf_op jit(solution)/shard_map/all_gather | solution.py:219
  468.8 21.2 %all-gather.21.cloned.1.call-done = bf16[1024,768]{1,0:T(8,128)(2,1)} async-done(((bf16[512,768]{1,0:T(8,128)(2,1)}), bf16[1024,768]{1,0:T(8,128)(2,1)}) %all-gather.21.cloned.1.call-update) | async-done | bytes 1572880 | tf_op jit(solution)/shard_map/all_gather | solution.py:219
  519.7 19.2 %reduce-scatter.33.cloned.1.call-done = bf16[512,768]{1,0:T(8,128)(2,1)} async-done(((bf16[1024,768]{1,0:T(8,128)(2,1)}), bf16[512,768]{1,0:T(8,128)(2,1)}) %reduce-scatter.33.cloned.1.call-update) | async-done | bytes 786448 | tf_op jit(solution)/shard_map/reduce_scatter | solution.py:225
  538.9 28.8 %reduce-scatter.29.cloned.1.call-done = bf16[512,768]{1,0:T(8,128)(2,1)} async-done(((bf16[1024,768]{1,0:T(8,128)(2,1)}), bf16[512,768]{1,0:T(8,128)(2,1)}) %reduce-scatter.29.cloned.1.call-update) | async-done | bytes 786448 | tf_op jit(solution)/shard_map/reduce_scatter | solution.py:225
  578.0 26.1 %all-gather.23.cloned.1.call-done = bf16[1024,768]{1,0:T(8,128)(2,1)} async-done(((bf16[512,768]{1,0:T(8,128)(2,1)}), bf16[1024,768]{1,0:T(8,128)(2,1)}) %all-gather.23.cloned.1.call-update) | async-done | bytes 1572880 | tf_op jit(solution)/shard_map/all_gather | solution.py:234
  609.1 82.4 %while.58 = (s32[]{:T(128)}, bf16[6,1024,64]{1,2,0:T(8,128)(2,1)S(1)}, bf16[6,1024,64]{1,2,0:T(8,128)(2,1)}, bf16[6,1024,64]{1,2,0:T(8,128)(2,1)S(1)}, s32[6]{0:...) while((s32[]{:T(128)}, ...), condition=%wide.region_32.33_spmd.clone, body=%wide.region_29.32_spmd.clone.sunk | while | flops 681246720 | bytes 38957408 | solution.py:133
  704.0 88.5 %while.59 = (s32[]{:T(128)}, bf16[6,1024,64]{1,2,0:T(8,128)(2,1)}, bf16[6,1024,64]{1,2,0:T(8,128)(2,1)}, bf16[6,1024,64]{1,2,0:T(8,128)(2,1)}, s32[6]{0:T(128)S(...) while((s32[]{:T(128)}, bf16[6,1024,64]{1,2,0:T(8,128)(2,1)}, ...), condition=%wide.region_42.43_spmd.clone, body=%wide.region_39.42_spmd.clone.sunk | while | flops 681246720 | bytes 38957408 | solution.py:133
  851.0 40.4 %all-reduce = (f32[768]{0:T(1024)}, f32[768]{0:T(1024)}, f32[768]{0:T(1024)}, f32[3072]{0:T(1024)}, f32[768]{0:T(1024)}, /*index=5*/f32[768]{0:T(1024)}, f32[768]{0:T(1024)}, f32[768]{0:T(1024)}, f32[768]{0:T(1024)}) all-reduce(f32[768]{0:T(1024)S(1)} %dynamic_update_slice.42, ...), channel_id=1, replica_groups=mesh['dp'=16,'tensor'=2] {'dp','tensor'}, use_global_device_ids=true, to_apply=%region_58.59 | all-reduce | flops 9216 | bytes 73728 | tf_op jit(solution)/shard_map/psum | solution.py:297
  896.5 52.1 %reduce-scatter.47.cloned.1.call-done = f32[48,384]{1,0:T(8,128)} async-done(((f32[768,384]{1,0:T(8,128)}), f32[48,384]{1,0:T(8,128)}) %reduce-scatter.47.cloned.1.call-update) | async-done | bytes 73744
  948.5 61.3 %reduce-scatter.43.cloned.1.call-done = f32[48,384]{1,0:T(8,128)} async-done(((f32[768,384]{1,0:T(8,128)}), f32[48,384]{1,0:T(8,128)}) %reduce-scatter.43.cloned.1.call-update) | async-done | bytes 73744
  1009.8 61.1 %reduce-scatter.45.cloned.1.call-done = f32[48,384]{1,0:T(8,128)} async-done(((f32[768,384]{1,0:T(8,128)}), f32[48,384]{1,0:T(8,128)}) %reduce-scatter.45.cloned.1.call-update) | async-done | bytes 73744
  1071.0 78.9 %reduce-scatter.41.cloned.1.call-done = f32[48,1536]{1,0:T(8,128)} async-done(((f32[768,1536]{1,0:T(8,128)}), f32[48,1536]{1,0:T(8,128)}) %reduce-scatter.41.cloned.1.call-update) | async-done | bytes 294928 | tf_op jit(solution)/shard_map/reduce_scatter | solution.py:54
  1149.8 79.4 %reduce-scatter.39.cloned.1.call-done = f32[48,1536]{1,0:T(8,128)} async-done(((f32[768,1536]{1,0:T(8,128)}), f32[48,1536]{1,0:T(8,128)}) %reduce-scatter.39.cloned.1.call-update) | async-done | bytes 294928 | tf_op jit(solution)/shard_map/reduce_scatter | solution.py:53
  (696 shorter events, 449.9 us)
Async XLA Ops:
  8.1 89.0 %all-gather.29.cloned.1.call-start = ((), (), s32[]{:S(2)}) async-start(), calls=%async_computation.30 | async-start | bytes 2359296 | tf_op jit(solution)/shard_map/all_gather | solution.py:187
  10.8 157.9 %all-gather.31.cloned.1.call-start = ((), (), s32[]{:S(2)}) async-start(), calls=%async_computation.31 | async-start | bytes 2359296 | tf_op jit(solution)/shard_map/all_gather | solution.py:187
  11.5 203.0 %reduce-scatter.21.cloned.1.call-start = ((), (), s32[]{:S(2)}) async-start(), calls=%async_computation.14 | async-start | bytes 4718592 | tf_op jit(solution)/shard_map/reduce_scatter | solution.py:192
  168.1 87.8 %reduce-scatter.25.cloned.1.call-start = ((), (), s32[]{:S(2)}) async-start(), calls=%async_computation.19 | async-start | bytes 4718592 | tf_op jit(solution)/shard_map/reduce_scatter | solution.py:192
  213.9 49.4 %all-gather.15.cloned.1.call-start = ((), (), s32[]{:S(2)}) async-start(), calls=%async_computation.16 | async-start | bytes 2506752 | tf_op jit(solution)/shard_map/all_gather | solution.py:42
  214.4 74.3 %all-gather.19.cloned.1.call-start = ((), (), s32[]{:S(2)}) async-start(), calls=%async_computation.20 | async-start | bytes 2359296 | tf_op jit(solution)/shard_map/all_gather | solution.py:203
  261.6 56.2 %all-gather.13.cloned.1.call-start = ((), (), s32[]{:S(2)}) async-start(), calls=%async_computation.15 | async-start | bytes 2359296 | tf_op jit(solution)/shard_map/all_gather | solution.py:203
  262.2 100.7 %all-gather.17.cloned.1.call-start = ((), (), s32[]{:S(2)}) async-start(), calls=%async_computation.17 | async-start | bytes 2506752 | tf_op jit(solution)/shard_map/all_gather | solution.py:43
  263.0 131.0 %reduce-scatter.23.cloned.1.call-start = ((), (), s32[]{:S(2)}) async-start(), calls=%async_computation.18 | async-start | bytes 2359296 | tf_op jit(solution)/shard_map/reduce_scatter | solution.py:207
  369.3 53.5 %reduce-scatter.27.cloned.1.call-start = ((), (), s32[]{:S(2)}) async-start(), calls=%async_computation.21 | async-start | bytes 2359296 | tf_op jit(solution)/shard_map/reduce_scatter | solution.py:207
  375.8 85.5 %all-gather.25.cloned.1.call-start = ((), (), s32[]{:S(2)}) async-start(), calls=%async_computation.26 | async-start | bytes 2359296 | tf_op jit(solution)/shard_map/all_gather | solution.py:219
  434.0 56.0 %all-gather.21.cloned.1.call-start = ((), (), s32[]{:S(2)}) async-start(), calls=%async_computation.22 | async-start | bytes 2359296 | tf_op jit(solution)/shard_map/all_gather | solution.py:219
  436.5 102.4 %reduce-scatter.33.cloned.1.call-start = ((), (), s32[]{:S(2)}) async-start(), calls=%async_computation.27 | async-start | bytes 2359296 | tf_op jit(solution)/shard_map/reduce_scatter | solution.py:225
  512.8 54.9 %reduce-scatter.29.cloned.1.call-start = ((), (), s32[]{:S(2)}) async-start(), calls=%async_computation.23 | async-start | bytes 2359296 | tf_op jit(solution)/shard_map/reduce_scatter | solution.py:225
  519.3 84.9 %all-gather.23.cloned.1.call-start = ((), (), s32[]{:S(2)}) async-start(), calls=%async_computation.24 | async-start | bytes 2359296 | tf_op jit(solution)/shard_map/all_gather | solution.py:234
  576.8 120.9 %all-gather.27.cloned.1.call-start = ((), (), s32[]{:S(2)}) async-start(), calls=%async_computation.28 | async-start | bytes 2359296 | tf_op jit(solution)/shard_map/all_gather | solution.py:234
  578.0 313.4 %reduce-scatter.31.cloned.1.call-start = ((), (), s32[]{:S(2)}) async-start(), calls=%async_computation.25 | async-start | bytes 2359296 | tf_op jit(solution)/shard_map/reduce_scatter | solution.py:251
  697.5 196.2 %reduce-scatter.35.cloned.1.call-start = ((), (), s32[]{:S(2)}) async-start(), calls=%async_computation.29 | async-start | bytes 2359296 | tf_op jit(solution)/shard_map/reduce_scatter | solution.py:251
  798.5 97.9 %reduce-scatter.37.cloned.1.call-start = ((), (), s32[]{:S(2)}) async-start(), calls=%async_computation.32 | async-start | bytes 1253376 | tf_op jit(solution)/shard_map/reduce_scatter | solution.py:52
  803.3 145.2 %reduce-scatter.47.cloned.1.call-start = ((), (), s32[]{:S(2)}) async-start(), calls=%async_computation.37 | async-start | bytes 1253376
  811.1 198.7 %reduce-scatter.43.cloned.1.call-start = ((), (), s32[]{:S(2)}) async-start(), calls=%async_computation.35 | async-start | bytes 1253376
  818.1 252.8 %reduce-scatter.45.cloned.1.call-start = ((), (), s32[]{:S(2)}) async-start(), calls=%async_computation.36 | async-start | bytes 1253376
  825.3 324.5 %reduce-scatter.41.cloned.1.call-start = ((), (), s32[]{:S(2)}) async-start(), calls=%async_computation.34 | async-start | bytes 5013504 | tf_op jit(solution)/shard_map/reduce_scatter | solution.py:54
  834.7 394.5 %reduce-scatter.39.cloned.1.call-start = ((), (), s32[]{:S(2)}) async-start(), calls=%async_computation.33 | async-start | bytes 5013504 | tf_op jit(solution)/shard_map/reduce_scatter | solution.py:53
  (101 other events, 1186.9 us)
Sparse Core Ops, SparseCore 0:
  11.0 29.8 all-gather.28
  43.1 27.2 all-gather.30
  168.2 41.9 reduce-scatter.20
  214.0 41.8 reduce-scatter.24
  434.1 27.2 all-gather.24
  462.7 27.2 all-gather.20
  576.9 27.1 all-gather.22
  606.3 27.2 all-gather.26
  697.6 26.0 reduce-scatter.30
  798.7 26.0 reduce-scatter.34
  829.0 58.2 reduce-scatter.36
  891.4 57.1 reduce-scatter.46
  952.7 57.0 reduce-scatter.42
  1013.9 57.0 reduce-scatter.44
  1075.2 74.5 reduce-scatter.40
  1154.6 74.5 reduce-scatter.38
Sparse Core Ops, SparseCore 1:
  216.6 41.0 all-gather.14
  261.7 27.0 all-gather.18
  290.8 27.0 all-gather.12
  320.2 42.7 all-gather.16
  369.4 24.5 reduce-scatter.22
  396.9 25.9 reduce-scatter.26
  512.9 26.0 reduce-scatter.32
  541.7 25.9 reduce-scatter.28
where the time goes:
time: 1250 us; the launch traced here: 1240 us
  waiting for transfers between devices  602 us (48%)
  matrix products  309 us (25%)
  blocking collectives  125 us (10%)
  other arithmetic  78.2 us (6%)
  local copies, waits for them, and re-layouts  60.7 us (5%)
  loops' own time  41.5 us (3%)
  between operations  16.9 us (1%)
    unnamed x27, waiting for transfers between devices  177 us
    dot_general x60, matrix products, product(): return jnp.dot(left_side, right_side, preferred_element_type=jnp.float32)  121 us
    dot_general x84, matrix products, contract_last(): lax.dot_general(left_side, right_side, (((1,), (1,)), ((), ())), preferre...  120 us
    reduce_scatter x1, waiting for transfers between devices, reduce_weights(): lax.psum_scatter(grad_in, 'dp', scatter_dimension=0, tiled=True)  79.4 us
    reduce_scatter x1, waiting for transfers between devices, reduce_weights(): lax.psum_scatter(grad_back, 'dp', scatter_dimension=0, tiled=True)  78.9 us
    dot_general x60, matrix products, contract_first(): lax.dot_general(left_side, right_side, (((0,), (0,)), ((), ())), preferre...  68.4 us
    reduce_scatter x2, waiting for transfers between devices, per_device(): lax.psum_scatter(contract_last(grad_pre, full_in).astype(jnp.bfloat16), '...  47.9 us
    all_gather x2, waiting for transfers between devices, per_device(): lax.all_gather(normed_one.astype(jnp.bfloat16), 'tensor', axis=0, tiled=T...  47.2 us
  transfers between devices with their start and end apart: 24, of which 16 were waited for; matrix products, arithmetic and copies ran while one was open for 32% of the time, Pallas kernels for 0%

commit v1 on v0

--- a/solution.py
+++ b/solution.py
@@ -295,18 +295,21 @@
         small_sums[8],
     )
     totals = lax.psum(
-        (
-            small_vectors[0],
-            small_vectors[1],
-            small_vectors[2],
-            small_vectors[3],
-            small_vectors[4],
-            small_vectors[5],
-            small_vectors[6],
-            small_vectors[7],
-            small_vectors[8],
+        lax.psum(
+            (
+                small_vectors[0],
+                small_vectors[1],
+                small_vectors[2],
+                small_vectors[3],
+                small_vectors[4],
+                small_vectors[5],
+                small_vectors[6],
+                small_vectors[7],
+                small_vectors[8],
+            ),
+            "tensor",
         ),
-        ("dp", "tensor"),
+        "dp",
     )
     return (
         output_rows,

time: 1250 us -> 1240 us (level)
  waiting for transfers between devices: 602 us -> 574 us
  blocking collectives: 125 us -> 152 us
    psum x0 -> x1, blocking collectives: none -> 60.5 us  [per_device(): lax.psum(lax.psum((small_vectors[0], small_vectors[1], small_vectors[2],...]
    psum x1, blocking collectives: 40.4 us -> 7.15 us  [per_device(): lax.psum((small_vectors[0], small_vectors[1], small_vectors[2], small_vec...]
    unnamed x27, waiting for transfers between devices: 177 us -> 150 us
where the time goes in v1:
time: 1240 us; the launch traced here: 1230 us
  waiting for transfers between devices  574 us (46%)
  matrix products  309 us (25%)
  blocking collectives  152 us (12%)
  other arithmetic  78.3 us (6%)
  local copies, waits for them, and re-layouts  60.6 us (5%)
  loops' own time  39.9 us (3%)
  between operations  16.9 us (1%)
    unnamed x27, waiting for transfers between devices  150 us
    dot_general x60, matrix products, product(): return jnp.dot(left_side, right_side, preferred_element_type=jnp.float32)  121 us
    dot_general x84, matrix products, contract_last(): lax.dot_general(left_side, right_side, (((1,), (1,)), ((), ())), preferre...  120 us
    reduce_scatter x1, waiting for transfers between devices, reduce_weights(): lax.psum_scatter(grad_in, 'dp', scatter_dimension=0, tiled=True)  79.4 us
    reduce_scatter x1, waiting for transfers between devices, reduce_weights(): lax.psum_scatter(grad_back, 'dp', scatter_dimension=0, tiled=True)  78.9 us
    dot_general x60, matrix products, contract_first(): lax.dot_general(left_side, right_side, (((0,), (0,)), ((), ())), preferre...  68.5 us
    psum x1, blocking collectives, per_device(): lax.psum(lax.psum((small_vectors[0], small_vectors[1], small_vectors[2],...  60.5 us
    reduce_scatter x2, waiting for transfers between devices, per_device(): lax.psum_scatter(contract_last(grad_pre, full_in).astype(jnp.bfloat16), '...  47.9 us
  transfers between devices with their start and end apart: 24, of which 16 were waited for; matrix products, arithmetic and copies ran while one was open for 32% of the time, Pallas kernels for 0%

profile of v1, /device:TPU:0, one launch (start us, length us, event | category | flops | bytes accessed | tf_op | source)
XLA Modules:
  0.0 1235.0 jit_solution(2151890974121110208)
XLA Ops:
  12.3 24.8 %all_gather.49 = bf16[768,384]{1,0:T(8,128)(2,1)S(1)} all-gather(bf16[48,384]{1,0:T(8,128)(2,1)S(1)} %copy-done.51), channel_id=1, replica_groups=mesh['dp'=16,'tensor'=2] {'dp'}, dimensions={0}, use_global_device_ids=true | all-gather | bytes 626688 | tf_op jit(solution)/shard_map/all_gather | solution.py:38
  37.1 19.0 %all_gather.50 = bf16[768,384]{1,0:T(8,128)(2,1)S(1)} all-gather(bf16[48,384]{1,0:T(8,128)(2,1)S(1)} %copy-done.52), channel_id=1, replica_groups=mesh['dp'=16,'tensor'=2] {'dp'}, dimensions={0}, use_global_device_ids=true | all-gather | bytes 626688 | tf_op jit(solution)/shard_map/all_gather | solution.py:39
  56.2 20.4 %all_gather.51 = bf16[768,384]{1,0:T(8,128)(2,1)S(1)} all-gather(bf16[48,384]{1,0:T(8,128)(2,1)S(1)} %copy-done.53), channel_id=1, replica_groups=mesh['dp'=16,'tensor'=2] {'dp'}, dimensions={0}, use_global_device_ids=true | all-gather | bytes 626688 | tf_op jit(solution)/shard_map/all_gather | solution.py:40
  76.6 20.4 %all_gather.52 = bf16[768,384]{1,0:T(8,128)(2,1)} all-gather(bf16[48,384]{1,0:T(8,128)(2,1)S(1)} %copy-done.54), channel_id=1, replica_groups=mesh['dp'=16,'tensor'=2] {'dp'}, dimensions={0}, use_global_device_ids=true | all-gather | bytes 626688 | tf_op jit(solution)/shard_map/all_gather | solution.py:41
  103.2 60.0 %while.56 = (s32[]{:T(128)}, bf16[6,1024,64]{1,2,0:T(8,128)(2,1)}, f32[6,1024]{1,0:T(8,128)}, s32[6]{0:T(128)S(1)}, bf16[1024,384]{1,0:T(8,128)(2,1)S(1)}, /*ind...) while((s32[]{:T(128)}, bf16[6,1024,64]{1,2,0:T(8,128)(2,1)}, ...), condition=%wide.region_5.6_spmd.clone, body=%wide.region_0.5_spmd.clone.sunk | while | flops 281281536 | bytes 14344927 | solution.py:92
  173.7 35.8 %while.57 = (s32[]{:T(128)}, bf16[6,1024,64]{1,2,0:T(8,128)(2,1)S(1)}, f32[6,1024]{1,0:T(8,128)S(1)}, s32[6]{0:T(128)S(1)}, bf16[1024,384]{1,0:T(8,128)(2,1)S(1)...) while((s32[]{:T(128)}, ...), condition=%wide.region_17.18_spmd.clone, body=%wide.region_12.0_spmd.clone.sunk | while | flops 281281536 | bytes 14344927 | solution.py:92
  214.5 41.4 %reduce-scatter.25.cloned.1.call-done = f32[512,768]{1,0:T(8,128)} async-done(((f32[1024,768]{1,0:T(8,128)}), f32[512,768]{1,0:T(8,128)}) %reduce-scatter.25.cloned.1.call-update) | async-done | bytes 1572880 | tf_op jit(solution)/shard_map/reduce_scatter | solution.py:192
  263.3 25.5 %all-gather.19.cloned.1.call-done = bf16[1024,768]{1,0:T(8,128)(2,1)} async-done(((bf16[512,768]{1,0:T(8,128)(2,1)}), bf16[1024,768]{1,0:T(8,128)(2,1)}) %all-gather.19.cloned.1.call-update) | async-done | bytes 1572880 | tf_op jit(solution)/shard_map/all_gather | solution.py:203
  296.2 21.7 %all-gather.13.cloned.1.call-done = bf16[1024,768]{1,0:T(8,128)(2,1)} async-done(((bf16[512,768]{1,0:T(8,128)(2,1)}), bf16[1024,768]{1,0:T(8,128)(2,1)}) %all-gather.13.cloned.1.call-update) | async-done | bytes 1572880 | tf_op jit(solution)/shard_map/all_gather | solution.py:203
  317.8 32.9 %multiply_convert_fusion.5 = (bf16[1024,1536]{1,0:T(8,128)(2,1)}, f32[1024,1536]{1,0:T(8,128)}, bf16[1024,1536]{1,0:T(8,128)(2,1)}, f32[1024,1536]{1,0:T(8,128)}, f32[1024,1536]{1,0:T(8,128)}) fusion(f32[1536]{0:T(1024)S(1)} %dynamic_slice.72, f32[1024,1536]{1,0:T(8,128)} %fusion.246, bf16[1024,768]{1,0:T(8,128)(2,1)} %all-gather.13.cloned.1.call-done, ...), kind=kOutput, calls=%fused_computation.195 | convolution fusion | flops 2623537152 | bytes 35395584 | tf_op jit(solution)/shard_map/dot_general | solution.py:21
  393.9 28.9 %reduce-scatter.27.cloned.1.call-done = bf16[512,768]{1,0:T(8,128)(2,1)} async-done(((bf16[1024,768]{1,0:T(8,128)(2,1)}), bf16[512,768]{1,0:T(8,128)(2,1)}) %reduce-scatter.27.cloned.1.call-update) | async-done | bytes 786448 | tf_op jit(solution)/shard_map/reduce_scatter | solution.py:207
  436.6 24.8 %all-gather.25.cloned.1.call-done = bf16[1024,768]{1,0:T(8,128)(2,1)} async-done(((bf16[512,768]{1,0:T(8,128)(2,1)}), bf16[1024,768]{1,0:T(8,128)(2,1)}) %all-gather.25.cloned.1.call-update) | async-done | bytes 1572880 | tf_op jit(solution)/shard_map/all_gather | solution.py:219
  468.8 21.2 %all-gather.21.cloned.1.call-done = bf16[1024,768]{1,0:T(8,128)(2,1)} async-done(((bf16[512,768]{1,0:T(8,128)(2,1)}), bf16[1024,768]{1,0:T(8,128)(2,1)}) %all-gather.21.cloned.1.call-update) | async-done | bytes 1572880 | tf_op jit(solution)/shard_map/all_gather | solution.py:219
  519.7 19.1 %reduce-scatter.33.cloned.1.call-done = bf16[512,768]{1,0:T(8,128)(2,1)} async-done(((bf16[1024,768]{1,0:T(8,128)(2,1)}), bf16[512,768]{1,0:T(8,128)(2,1)}) %reduce-scatter.33.cloned.1.call-update) | async-done | bytes 786448 | tf_op jit(solution)/shard_map/reduce_scatter | solution.py:225
  538.9 28.8 %reduce-scatter.29.cloned.1.call-done = bf16[512,768]{1,0:T(8,128)(2,1)} async-done(((bf16[1024,768]{1,0:T(8,128)(2,1)}), bf16[512,768]{1,0:T(8,128)(2,1)}) %reduce-scatter.29.cloned.1.call-update) | async-done | bytes 786448 | tf_op jit(solution)/shard_map/reduce_scatter | solution.py:225
  578.1 26.1 %all-gather.23.cloned.1.call-done = bf16[1024,768]{1,0:T(8,128)(2,1)} async-done(((bf16[512,768]{1,0:T(8,128)(2,1)}), bf16[1024,768]{1,0:T(8,128)(2,1)}) %all-gather.23.cloned.1.call-update) | async-done | bytes 1572880 | tf_op jit(solution)/shard_map/all_gather | solution.py:234
  609.1 80.6 %while.58 = (s32[]{:T(128)}, bf16[6,1024,64]{1,2,0:T(8,128)(2,1)S(1)}, bf16[6,1024,64]{1,2,0:T(8,128)(2,1)}, bf16[6,1024,64]{1,2,0:T(8,128)(2,1)S(1)}, s32[6]{0:...) while((s32[]{:T(128)}, ...), condition=%wide.region_32.33_spmd.clone, body=%wide.region_29.32_spmd.clone.sunk | while | flops 681246720 | bytes 38957408 | solution.py:133
  702.4 88.6 %while.59 = (s32[]{:T(128)}, bf16[6,1024,64]{1,2,0:T(8,128)(2,1)}, bf16[6,1024,64]{1,2,0:T(8,128)(2,1)}, bf16[6,1024,64]{1,2,0:T(8,128)(2,1)}, s32[6]{0:T(128)S(...) while((s32[]{:T(128)}, bf16[6,1024,64]{1,2,0:T(8,128)(2,1)}, ...), condition=%wide.region_42.43_spmd.clone, body=%wide.region_39.42_spmd.clone.sunk | while | flops 681246720 | bytes 38957408 | solution.py:133
  856.7 60.5 %all-reduce = (f32[768]{0:T(1024)}, f32[768]{0:T(1024)}, f32[768]{0:T(1024)}, f32[3072]{0:T(1024)}, f32[768]{0:T(1024)}, /*index=5*/f32[768]{0:T(1024)}, f32[768]{0:T(1024)}, f32[768]{0:T(1024)}, f32[768]{0:T(1024)}) all-reduce(f32[768]{0:T(1024)S(1)} %get-tuple-element.458, ...), channel_id=1, replica_groups=mesh['dp'=16,'tensor'=2] {'dp'}, use_global_device_ids=true, to_apply=%region_59.60 | all-reduce | flops 9216 | bytes 73728 | tf_op jit(solution)/shard_map/psum | solution.py:297
  922.2 24.5 %reduce-scatter.47.cloned.1.call-done = f32[48,384]{1,0:T(8,128)} async-done(((f32[768,384]{1,0:T(8,128)}), f32[48,384]{1,0:T(8,128)}) %reduce-scatter.47.cloned.1.call-update) | async-done | bytes 73744
  946.8 61.4 %reduce-scatter.43.cloned.1.call-done = f32[48,384]{1,0:T(8,128)} async-done(((f32[768,384]{1,0:T(8,128)}), f32[48,384]{1,0:T(8,128)}) %reduce-scatter.43.cloned.1.call-update) | async-done | bytes 73744
  1008.1 61.2 %reduce-scatter.45.cloned.1.call-done = f32[48,384]{1,0:T(8,128)} async-done(((f32[768,384]{1,0:T(8,128)}), f32[48,384]{1,0:T(8,128)}) %reduce-scatter.45.cloned.1.call-update) | async-done | bytes 73744
  1069.3 78.9 %reduce-scatter.41.cloned.1.call-done = f32[48,1536]{1,0:T(8,128)} async-done(((f32[768,1536]{1,0:T(8,128)}), f32[48,1536]{1,0:T(8,128)}) %reduce-scatter.41.cloned.1.call-update) | async-done | bytes 294928 | tf_op jit(solution)/shard_map/reduce_scatter | solution.py:54
  1148.2 79.4 %reduce-scatter.39.cloned.1.call-done = f32[48,1536]{1,0:T(8,128)} async-done(((f32[768,1536]{1,0:T(8,128)}), f32[48,1536]{1,0:T(8,128)}) %reduce-scatter.39.cloned.1.call-update) | async-done | bytes 294928 | tf_op jit(solution)/shard_map/reduce_scatter | solution.py:53
  (697 shorter events, 457.2 us)
Async XLA Ops:
  8.1 89.0 %all-gather.29.cloned.1.call-start = ((), (), s32[]{:S(2)}) async-start(), calls=%async_computation.30 | async-start | bytes 2359296 | tf_op jit(solution)/shard_map/all_gather | solution.py:187
  10.8 157.9 %all-gather.31.cloned.1.call-start = ((), (), s32[]{:S(2)}) async-start(), calls=%async_computation.31 | async-start | bytes 2359296 | tf_op jit(solution)/shard_map/all_gather | solution.py:187
  11.5 203.0 %reduce-scatter.21.cloned.1.call-start = ((), (), s32[]{:S(2)}) async-start(), calls=%async_computation.14 | async-start | bytes 4718592 | tf_op jit(solution)/shard_map/reduce_scatter | solution.py:192
  168.1 87.8 %reduce-scatter.25.cloned.1.call-start = ((), (), s32[]{:S(2)}) async-start(), calls=%async_computation.19 | async-start | bytes 4718592 | tf_op jit(solution)/shard_map/reduce_scatter | solution.py:192
  213.8 49.4 %all-gather.15.cloned.1.call-start = ((), (), s32[]{:S(2)}) async-start(), calls=%async_computation.16 | async-start | bytes 2506752 | tf_op jit(solution)/shard_map/all_gather | solution.py:42
  214.4 74.4 %all-gather.19.cloned.1.call-start = ((), (), s32[]{:S(2)}) async-start(), calls=%async_computation.20 | async-start | bytes 2359296 | tf_op jit(solution)/shard_map/all_gather | solution.py:203
  261.6 56.2 %all-gather.13.cloned.1.call-start = ((), (), s32[]{:S(2)}) async-start(), calls=%async_computation.15 | async-start | bytes 2359296 | tf_op jit(solution)/shard_map/all_gather | solution.py:203
  262.2 100.7 %all-gather.17.cloned.1.call-start = ((), (), s32[]{:S(2)}) async-start(), calls=%async_computation.17 | async-start | bytes 2506752 | tf_op jit(solution)/shard_map/all_gather | solution.py:43
  262.9 131.0 %reduce-scatter.23.cloned.1.call-start = ((), (), s32[]{:S(2)}) async-start(), calls=%async_computation.18 | async-start | bytes 2359296 | tf_op jit(solution)/shard_map/reduce_scatter | solution.py:207
  369.3 53.5 %reduce-scatter.27.cloned.1.call-start = ((), (), s32[]{:S(2)}) async-start(), calls=%async_computation.21 | async-start | bytes 2359296 | tf_op jit(solution)/shard_map/reduce_scatter | solution.py:207
  375.8 85.5 %all-gather.25.cloned.1.call-start = ((), (), s32[]{:S(2)}) async-start(), calls=%async_computation.26 | async-start | bytes 2359296 | tf_op jit(solution)/shard_map/all_gather | solution.py:219
  434.0 56.0 %all-gather.21.cloned.1.call-start = ((), (), s32[]{:S(2)}) async-start(), calls=%async_computation.22 | async-start | bytes 2359296 | tf_op jit(solution)/shard_map/all_gather | solution.py:219
  436.5 102.4 %reduce-scatter.33.cloned.1.call-start = ((), (), s32[]{:S(2)}) async-start(), calls=%async_computation.27 | async-start | bytes 2359296 | tf_op jit(solution)/shard_map/reduce_scatter | solution.py:225
  512.8 54.9 %reduce-scatter.29.cloned.1.call-start = ((), (), s32[]{:S(2)}) async-start(), calls=%async_computation.23 | async-start | bytes 2359296 | tf_op jit(solution)/shard_map/reduce_scatter | solution.py:225
  519.3 84.9 %all-gather.23.cloned.1.call-start = ((), (), s32[]{:S(2)}) async-start(), calls=%async_computation.24 | async-start | bytes 2359296 | tf_op jit(solution)/shard_map/all_gather | solution.py:234
  576.8 119.2 %all-gather.27.cloned.1.call-start = ((), (), s32[]{:S(2)}) async-start(), calls=%async_computation.28 | async-start | bytes 2359296 | tf_op jit(solution)/shard_map/all_gather | solution.py:234
  578.0 339.1 %reduce-scatter.31.cloned.1.call-start = ((), (), s32[]{:S(2)}) async-start(), calls=%async_computation.25 | async-start | bytes 2359296 | tf_op jit(solution)/shard_map/reduce_scatter | solution.py:251
  695.8 223.7 %reduce-scatter.35.cloned.1.call-start = ((), (), s32[]{:S(2)}) async-start(), calls=%async_computation.29 | async-start | bytes 2359296 | tf_op jit(solution)/shard_map/reduce_scatter | solution.py:251
  796.9 125.3 %reduce-scatter.37.cloned.1.call-start = ((), (), s32[]{:S(2)}) async-start(), calls=%async_computation.32 | async-start | bytes 1253376 | tf_op jit(solution)/shard_map/reduce_scatter | solution.py:52
  801.7 145.1 %reduce-scatter.47.cloned.1.call-start = ((), (), s32[]{:S(2)}) async-start(), calls=%async_computation.37 | async-start | bytes 1253376
  809.5 198.6 %reduce-scatter.43.cloned.1.call-start = ((), (), s32[]{:S(2)}) async-start(), calls=%async_computation.35 | async-start | bytes 1253376
  816.6 252.7 %reduce-scatter.45.cloned.1.call-start = ((), (), s32[]{:S(2)}) async-start(), calls=%async_computation.36 | async-start | bytes 1253376
  823.7 324.5 %reduce-scatter.41.cloned.1.call-start = ((), (), s32[]{:S(2)}) async-start(), calls=%async_computation.34 | async-start | bytes 5013504 | tf_op jit(solution)/shard_map/reduce_scatter | solution.py:54
  833.1 394.5 %reduce-scatter.39.cloned.1.call-start = ((), (), s32[]{:S(2)}) async-start(), calls=%async_computation.33 | async-start | bytes 5013504 | tf_op jit(solution)/shard_map/reduce_scatter | solution.py:53
  (101 other events, 1296.5 us)
Sparse Core Ops, SparseCore 0:
  11.0 29.8 all-gather.28
  43.1 27.2 all-gather.30
  168.2 41.9 reduce-scatter.20
  214.0 41.9 reduce-scatter.24
  434.1 27.1 all-gather.24
  462.7 27.2 all-gather.20
  577.0 27.2 all-gather.22
  606.3 27.1 all-gather.26
  695.9 26.1 reduce-scatter.30
  797.1 26.0 reduce-scatter.34
  827.4 58.0 reduce-scatter.36
  889.5 57.2 reduce-scatter.46
  950.9 57.1 reduce-scatter.42
  1012.2 57.1 reduce-scatter.44
  1073.6 74.5 reduce-scatter.40
  1153.0 74.5 reduce-scatter.38
Sparse Core Ops, SparseCore 1:
  216.6 41.0 all-gather.14
  261.7 27.0 all-gather.18
  290.8 27.0 all-gather.12
  320.2 42.7 all-gather.16
  369.4 24.5 reduce-scatter.22
  396.9 25.9 reduce-scatter.26
  512.9 25.9 reduce-scatter.32
  541.7 25.9 reduce-scatter.28
